TPU v7x, 512 devices: a whole 4x8x8 slice. The times are simulated.
512 devices in a mesh: dp: 8 (over z_lo, core), seq: 64 (over z_hi, y, x).
Axes of the slice: x: 4, y: 8, z: 8 (z_hi: 2, z_lo: 4; z = z_hi * 4 + z_lo), core: 2. Of those that a mesh axis runs over, the one named last changes fastest.
Arguments:
- value_branch: bfloat16 [512, 65536], P(None, ('dp', 'seq')), parts along dimension 1, may hold values from -6 to 6
- first_gate: bfloat16 [512, 65536], P(None, ('dp', 'seq')), parts along dimension 1, may hold values from -6 to 6
- second_gate: bfloat16 [512, 65536], P(None, ('dp', 'seq')), parts along dimension 1, may hold values from -6 to 6
- out_cotangent: bfloat16 [512, 65536], P(None, ('dp', 'seq')), parts along dimension 1, may hold values from -6 to 6
- pos_weight: float32 [64, 33], replicated, may hold values from -4 to 4
- pos_bias: float32 [64], replicated, may hold values from -3.140625 to 3.140625
- mid_weight: float32 [64, 64], replicated, may hold values from -0.75 to 0.75
- mid_bias: float32 [64], replicated, may hold values from -3.140625 to 3.140625
- out_weight: float32 [1024, 64], replicated, may hold values from -0.0234375 to 0.0234375
- decay_rates: float32 [1024], replicated, may hold values from 3.07 to 15.35
Outputs:
- value_grad: bfloat16 [512, 65536], P(None, ('dp', 'seq')), parts along dimension 1
- first_gate_grad: bfloat16 [512, 65536], P(None, ('dp', 'seq')), parts along dimension 1
- second_gate_grad: bfloat16 [512, 65536], P(None, ('dp', 'seq')), parts along dimension 1
- pos_weight_grad: float32 [512, 33], P('dp'), parts along dimension 0
- pos_bias_grad: float32 [512], P('dp'), parts along dimension 0
- mid_weight_grad: float32 [512, 64], P('dp'), parts along dimension 0
- mid_bias_grad: float32 [512], P('dp'), parts along dimension 0
- out_weight_grad: float32 [1024, 512], P('seq', 'dp'), parts along dimension 1
There are 8 independent parts, one for each index of `dp`. A program takes and returns all parts, laid end to end along the dimension named above; an argument that names none is the same for every part. Nothing has to cross between parts.
All inputs are finite; a program needn't handle non-finite values.
Results may differ from a plain program's by a relative error of at most 0.017.
Values may be sent and summed in bfloat16 or wider, within the bound.
No kernel may reach another device: no remote copies, remote signals or barrier semaphores. Data moves between devices by JAX's collectives and lax.ppermute only.
A program may use at most 64 MiB of HBM per device.

v0:
```python
import math
import jax
import jax.numpy as jnp
from jax import lax
from jax.sharding import PartitionSpec as P

RADIX = 128


def make_tables(freq_rows, radix):
    length_all = freq_rows * radix
    freq_index = jnp.arange(freq_rows, dtype=jnp.int32)
    half_index = jnp.arange(freq_rows // 2, dtype=jnp.int32)
    inner_index = jnp.arange(radix, dtype=jnp.int32)
    angle_one = (freq_index[:, None] * half_index[None, :] % freq_rows).astype(jnp.float32) * (
        2.0 * math.pi / freq_rows
    )
    angle_two = (inner_index[:, None] * inner_index[None, :] % radix).astype(jnp.float32) * (
        2.0 * math.pi / radix
    )
    angle_twid = (freq_index[:, None] * inner_index[None, :] % length_all).astype(jnp.float32) * (
        2.0 * math.pi / length_all
    )
    cos_one = jnp.cos(angle_one).astype(jnp.bfloat16)
    sin_one = jnp.sin(angle_one).astype(jnp.bfloat16)
    cos_two = jnp.cos(angle_two).astype(jnp.bfloat16)
    sin_two = jnp.sin(angle_two).astype(jnp.bfloat16)
    left_table = jnp.concatenate([cos_one, -sin_one], axis=0)
    right_fwd = jnp.concatenate(
        [jnp.concatenate([cos_two, -sin_two], axis=1), jnp.concatenate([sin_two, cos_two], axis=1)],
        axis=0,
    )
    right_inv = jnp.concatenate(
        [jnp.concatenate([cos_two, sin_two], axis=1), jnp.concatenate([-sin_two, cos_two], axis=1)],
        axis=0,
    )
    return (left_table, right_fwd, right_inv, jnp.cos(angle_twid), jnp.sin(angle_twid))


def forward_spectrum(signal, tables, freq_rows, radix):
    left_table, right_fwd, right_inv, twid_cos, twid_sin = tables
    count = signal.shape[0]
    shaped = signal.reshape(count, freq_rows // 2, radix)
    stacked = jnp.einsum("kn,rnm->rkm", left_table, shaped, preferred_element_type=jnp.float32)
    real_a = stacked[:, :freq_rows]
    imag_a = stacked[:, freq_rows:]
    real_b = (real_a * twid_cos + imag_a * twid_sin).astype(jnp.bfloat16)
    imag_b = (imag_a * twid_cos - real_a * twid_sin).astype(jnp.bfloat16)
    joined = jnp.concatenate([real_b, imag_b], axis=2)
    spectrum = jnp.einsum("rkn,nm->rkm", joined, right_fwd, preferred_element_type=jnp.float32)
    return (spectrum[:, :, :radix], spectrum[:, :, radix:])


def inverse_signal(product, tables, freq_rows, radix):
    left_table, right_fwd, right_inv, twid_cos, twid_sin = tables
    real_p, imag_p = product
    joined = jnp.concatenate([real_p, imag_p], axis=2)
    section_q = jnp.einsum("rkn,nm->rkm", joined, right_inv, preferred_element_type=jnp.float32)
    real_q = section_q[:, :, :radix]
    imag_q = section_q[:, :, radix:]
    real_r = (real_q * twid_cos - imag_q * twid_sin).astype(jnp.bfloat16)
    imag_r = (imag_q * twid_cos + real_q * twid_sin).astype(jnp.bfloat16)
    rows_both = jnp.concatenate([real_r, imag_r], axis=1)
    output = jnp.einsum("kn,rkm->rnm", left_table, rows_both, preferred_element_type=jnp.float32)
    count = real_p.shape[0]
    return (output * (1.0 / (freq_rows * radix))).reshape(count, freq_rows // 2 * radix)


def spectral_product(left, right, conj_left, conj_right):
    sign_left = -1.0 if conj_left else 1.0
    sign_right = -1.0 if conj_right else 1.0
    real_part = left[0] * right[0] - sign_left * sign_right * left[1] * right[1]
    imag_part = sign_left * left[1] * right[0] + sign_right * left[0] * right[1]
    return (real_part.astype(jnp.bfloat16), imag_part.astype(jnp.bfloat16))


def positional_features(positions, seq_len, bands):
    band_index = jnp.arange(1, bands + 1, dtype=jnp.int32)
    angles = (band_index[:, None] * positions[None, :] % seq_len).astype(jnp.float32) * (
        2.0 * math.pi / seq_len
    )
    ramp = positions.astype(jnp.float32)[None, :] / seq_len
    return jnp.concatenate([ramp, jnp.cos(angles), jnp.sin(angles)], axis=0)


def filter_network(positions, seq_len, pos_weight, pos_bias, mid_weight, mid_bias):
    bands = (pos_weight.shape[1] - 1) // 2
    features = positional_features(positions, seq_len, bands)
    pre_one = jnp.dot(pos_weight, features, precision=lax.Precision.HIGHEST) + pos_bias[:, None]
    act_one = jnp.sin(pre_one)
    pre_two = jnp.dot(mid_weight, act_one, precision=lax.Precision.HIGHEST) + mid_bias[:, None]
    act_two = jnp.sin(pre_two)
    return (features, pre_one, act_one, pre_two, act_two)


def modulation(rates, positions, seq_len):
    return jnp.exp(-rates[:, None] * positions.astype(jnp.float32)[None, :] / seq_len)


def contract_last(left, right):
    return lax.dot_general(left, right, (((1,), (1,)), ((), ())), precision=lax.Precision.HIGHEST)


def network_backward(act_grad, features, pre_one, act_one, pre_two, mid_weight):
    pre_two_grad = act_grad * jnp.cos(pre_two)
    mid_weight_part = contract_last(pre_two_grad, act_one)
    mid_bias_part = jnp.sum(pre_two_grad, axis=1)
    pre_one_grad = jnp.dot(mid_weight.T, pre_two_grad, precision=lax.Precision.HIGHEST) * jnp.cos(
        pre_one
    )
    pos_weight_part = contract_last(pre_one_grad, features)
    pos_bias_part = jnp.sum(pre_one_grad, axis=1)
    return (pos_weight_part, pos_bias_part, mid_weight_part, mid_bias_part)


def on_device(
    value_branch,
    first_gate,
    second_gate,
    out_cotangent,
    pos_weight,
    pos_bias,
    mid_weight,
    mid_bias,
    out_weight,
    decay_rates,
):
    model_width, tok_dev = value_branch.shape
    devices = lax.axis_size("seq")
    seq_len = tok_dev * devices
    channels = model_width // devices
    my_rank = lax.axis_index("seq")
    freq_rows = 2 * seq_len // RADIX
    tables = make_tables(freq_rows, RADIX)
    all_positions = jnp.arange(seq_len, dtype=jnp.int32)
    own_rates = lax.dynamic_slice_in_dim(decay_rates, my_rank * 2 * channels, 2 * channels)
    window_own = modulation(own_rates, all_positions, seq_len)
    value_ch, first_ch = (
        lax.all_to_all(value_branch, "seq", split_axis=0, concat_axis=1, tiled=True),
        lax.all_to_all(first_gate, "seq", split_axis=0, concat_axis=1, tiled=True),
    )
    local_positions = my_rank * tok_dev + jnp.arange(tok_dev, dtype=jnp.int32)
    features, pre_one, act_one, pre_two, act_two = filter_network(
        local_positions, seq_len, pos_weight, pos_bias, mid_weight, mid_bias
    )
    window_local = modulation(decay_rates, local_positions, seq_len)
    local_filters = (
        jnp.dot(out_weight, act_two, precision=lax.Precision.HIGHEST) * window_local
    ).astype(jnp.bfloat16)
    filt_ch = lax.all_to_all(local_filters, "seq", split_axis=0, concat_axis=1, tiled=True)
    filt_real, filt_imag = forward_spectrum(filt_ch, tables, freq_rows, RADIX)
    filt_real = filt_real.reshape(channels, 2, freq_rows, RADIX)
    filt_imag = filt_imag.reshape(channels, 2, freq_rows, RADIX)
    spec_one = (filt_real[:, 0], filt_imag[:, 0])
    spec_two = (filt_real[:, 1], filt_imag[:, 1])
    spec_val = forward_spectrum(value_ch, tables, freq_rows, RADIX)
    conv_one = inverse_signal(
        spectral_product(spec_one, spec_val, False, False), tables, freq_rows, RADIX
    )
    gated = (first_ch.astype(jnp.float32) * conv_one).astype(jnp.bfloat16)
    spec_gated = forward_spectrum(gated, tables, freq_rows, RADIX)
    conv_two = inverse_signal(
        spectral_product(spec_two, spec_gated, False, False), tables, freq_rows, RADIX
    )
    second_ch, cot_ch = (
        lax.all_to_all(second_gate, "seq", split_axis=0, concat_axis=1, tiled=True),
        lax.all_to_all(out_cotangent, "seq", split_axis=0, concat_axis=1, tiled=True),
    )
    cot_wide = cot_ch.astype(jnp.float32)
    second_grad_ch = (cot_wide * conv_two).astype(jnp.bfloat16)
    second_out = lax.all_to_all(second_grad_ch, "seq", split_axis=1, concat_axis=0, tiled=True)
    grad_two = (cot_wide * second_ch.astype(jnp.float32)).astype(jnp.bfloat16)
    spec_gtwo = forward_spectrum(grad_two, tables, freq_rows, RADIX)
    gated_grad = inverse_signal(
        spectral_product(spec_two, spec_gtwo, True, False), tables, freq_rows, RADIX
    )
    filt_grad_two = inverse_signal(
        spectral_product(spec_gtwo, spec_gated, False, True), tables, freq_rows, RADIX
    )
    first_grad_ch = (gated_grad * conv_one).astype(jnp.bfloat16)
    grad_one = (gated_grad * first_ch.astype(jnp.float32)).astype(jnp.bfloat16)
    spec_gone = forward_spectrum(grad_one, tables, freq_rows, RADIX)
    value_grad_ch = inverse_signal(
        spectral_product(spec_one, spec_gone, True, False), tables, freq_rows, RADIX
    ).astype(jnp.bfloat16)
    filt_grad_one = inverse_signal(
        spectral_product(spec_gone, spec_val, False, True), tables, freq_rows, RADIX
    )
    value_out, first_out = (
        lax.all_to_all(value_grad_ch, "seq", split_axis=1, concat_axis=0, tiled=True),
        lax.all_to_all(first_grad_ch, "seq", split_axis=1, concat_axis=0, tiled=True),
    )
    filt_grads = jnp.stack([filt_grad_one, filt_grad_two], axis=1).reshape(2 * channels, seq_len)
    filter_grad_ch = filt_grads * window_own / seq_len
    filter_grad_seq = lax.all_to_all(
        filter_grad_ch.astype(jnp.bfloat16), "seq", split_axis=1, concat_axis=0, tiled=True
    ).astype(filter_grad_ch.dtype)
    out_weight_grad = lax.psum_scatter(
        contract_last(filter_grad_seq, act_two), "seq", scatter_dimension=0, tiled=True
    )
    act_grad = jnp.dot(out_weight.T, filter_grad_seq, precision=lax.Precision.HIGHEST)
    partials = network_backward(act_grad, features, pre_one, act_one, pre_two, mid_weight)
    pos_weight_grad, pos_bias_grad, mid_weight_grad, mid_bias_grad = lax.psum(
        (partials[0], partials[1], partials[2], partials[3]), "seq"
    )
    return (
        value_out,
        first_out,
        second_out,
        pos_weight_grad,
        pos_bias_grad,
        mid_weight_grad,
        mid_bias_grad,
        out_weight_grad,
    )


def solution(mesh):
    in_specs = (
        P(None, ("dp", "seq")),
        P(None, ("dp", "seq")),
        P(None, ("dp", "seq")),
        P(None, ("dp", "seq")),
        P(),
        P(),
        P(),
        P(),
        P(),
        P(),
    )
    out_specs = (
        P(None, ("dp", "seq")),
        P(None, ("dp", "seq")),
        P(None, ("dp", "seq")),
        P("dp", None),
        P("dp"),
        P("dp", None),
        P("dp"),
        P("seq", "dp"),
    )
    return jax.shard_map(
        on_device, mesh=mesh, in_specs=in_specs, out_specs=out_specs, check_vma=False
    )
```

profile of v0, /device:TPU:64, one launch (start us, length us, event | category | flops | bytes accessed | tf_op | source)
XLA Modules:
  0.0 657.4 jit_solution(1359038051351091509)
XLA Ops:
  7.2 18.3 %all-to-all-start.1 = ((bf16[64,8,128]{2,1,0:T(8,128)(2,1)}), bf16[64,8,128]{2,1,0:T(8,128)(2,1)S(1)}, u32[]{:S(2)}, u32[]{:S(2)}) async-start(bf16[64,8,128]{2,1,0:T(8,128)(2,1)} %bitcast.181), calls=%async_computation.1 | async-start | bytes 262144 | tf_op jit(solution)/shard_map/all_to_all | solution.py:167
  26.4 1.6 fusion.148
  28.7 1.6 fusion.149
  30.3 10.2 %all-to-all-done.1 = bf16[64,8,128]{2,1,0:T(8,128)(2,1)S(1)} async-done(((bf16[64,8,128]{2,1,0:T(8,128)(2,1)}), bf16[64,8,128]{2,1,0:T(8,128)(2,1)S(1)}, u32[]{:S(2)}, u32[]{:S(2)}) %all-to-all-start.1) | async-done | bytes 131104 | tf_op jit(solution)/shard_map/all_to_all | solution.py:167
  40.5 5.0 all-to-all-start.5
  47.0 13.6 %all-to-all-done.5 = bf16[64,8,128]{2,1,0:T(8,128)(2,1)S(1)} async-done(((bf16[64,8,128]{2,1,0:T(8,128)(2,1)}), bf16[64,8,128]{2,1,0:T(8,128)(2,1)S(1)}, u32[]{:S(2)}, u32[]{:S(2)}) %all-to-all-start.5) | async-done | bytes 131104 | tf_op jit(solution)/shard_map/all_to_all | solution.py:139
  60.6 4.6 all-to-all-start.2
  66.8 13.5 %all-to-all-done.2 = bf16[64,8,128]{2,1,0:T(8,128)(2,1)S(1)} async-done(((bf16[64,8,128]{2,1,0:T(8,128)(2,1)}), bf16[64,8,128]{2,1,0:T(8,128)(2,1)S(1)}, u32[]{:S(2)}, u32[]{:S(2)}) %all-to-all-start.2) | async-done | bytes 131104 | tf_op jit(solution)/shard_map/all_to_all | solution.py:166
  80.3 4.6 all-to-all-start
  86.3 14.5 %all-to-all-done = bf16[64,16,128]{2,1,0:T(8,128)(2,1)S(1)} async-done(((bf16[64,16,128]{2,1,0:T(8,128)(2,1)}), bf16[64,16,128]{2,1,0:T(8,128)(2,1)S(1)}, u32[]{:S(2)}, u32[]{:S(2)}) %all-to-all-start) | async-done | bytes 262176 | tf_op jit(solution)/shard_map/all_to_all | solution.py:150
  100.8 5.6 all-to-all-start.3
  110.5 1.3 fusion.17
  111.8 9.3 %all-to-all-done.3 = bf16[64,8,128]{2,1,0:T(8,128)(2,1)} async-done(((bf16[64,8,128]{2,1,0:T(8,128)(2,1)}), bf16[64,8,128]{2,1,0:T(8,128)(2,1)}, u32[]{:S(2)}, u32[]{:S(2)}) %all-to-all-start.3) | async-done | bytes 131104 | tf_op jit(solution)/shard_map/all_to_all | solution.py:140
  121.1 1.4 convolution_bitcast_fusion.1
  131.4 5.6 all-to-all-start.7
  138.1 14.0 %all-to-all-done.7 = bf16[8,64,128]{2,0,1:T(8,128)(2,1)S(1)} async-done(((bf16[8,64,128]{2,0,1:T(8,128)(2,1)}), bf16[8,64,128]{2,0,1:T(8,128)(2,1)S(1)}, u32[]{:S(2)}, u32[]{:S(2)}) %all-to-all-start.7) | async-done | bytes 131104 | tf_op jit(solution)/shard_map/all_to_all | solution.py:171
  152.1 4.6 all-to-all-start.4
  158.8 12.9 %all-to-all-done.4 = bf16[8,64,128]{2,0,1:T(8,128)(2,1)S(1)} async-done(((bf16[8,64,128]{2,0,1:T(8,128)(2,1)}), bf16[8,64,128]{2,0,1:T(8,128)(2,1)S(1)}, u32[]{:S(2)}, u32[]{:S(2)}) %all-to-all-start.4) | async-done | bytes 131104 | tf_op jit(solution)/shard_map/all_to_all | solution.py:190
  171.7 4.6 all-to-all-start.6
  178.4 13.0 %all-to-all-done.6 = bf16[8,64,128]{2,0,1:T(8,128)(2,1)S(1)} async-done(((bf16[8,64,128]{2,0,1:T(8,128)(2,1)}), bf16[8,64,128]{2,0,1:T(8,128)(2,1)S(1)}, u32[]{:S(2)}, u32[]{:S(2)}) %all-to-all-start.6) | async-done | bytes 131104 | tf_op jit(solution)/shard_map/all_to_all | solution.py:191
  191.4 4.6 all-to-all-start.8
  196.1 15.7 %all-to-all-done.8 = bf16[16,64,128]{2,0,1:T(8,128)(2,1)S(1)} async-done(((bf16[16,64,128]{2,0,1:T(8,128)(2,1)}), bf16[16,64,128]{2,0,1:T(8,128)(2,1)S(1)}, u32[]{:S(2)}, u32[]{:S(2)}) %all-to-all-start.8) | async-done | bytes 262176 | tf_op jit(solution)/shard_map/all_to_all | solution.py:195
  214.1 429.3 %all-reduce = (f32[64,33]{0,1:T(8,128)}, f32[64]{0:T(128)}, f32[64,64]{1,0:T(8,128)}, f32[64]{0:T(128)}) all-reduce(f32[64,33]{0,1:T(8,128)S(1)} %fusion.109, f32[64]{0:T(128)S(1)} %get-tuple-element.70, f32[64,64]{1,0:T(8,128)S(1)} %fusion.152, f32[64]{0:T(128)S(1)} %get-tuple-element.72), channel_id=1, replica_groups=mesh['dp'=8,'seq'=64] {'seq'}, use_global_device_ids=true, to_apply=%region_0.1 | all-reduce | flops 6336 | bytes 50688 | tf_op jit(solution)/shard_map/psum | solution.py:203
  643.4 5.2 reduce-scatter.2.cloned.1.call-done
  (111 shorter events, 27.9 us)
Async XLA Ops:
  7.2 39.2 %copy-start = (f32[1024,64]{0,1:T(8,128)S(1)}, f32[1024,64]{0,1:T(8,128)}, u32[]{:S(2)}) copy-start(f32[1024,64]{0,1:T(8,128)} %param.18) | copy-start | bytes 786436
  7.2 33.3 %all-to-all-start.1 = ((bf16[64,8,128]{2,1,0:T(8,128)(2,1)}), bf16[64,8,128]{2,1,0:T(8,128)(2,1)S(1)}, u32[]{:S(2)}, u32[]{:S(2)}) async-start(bf16[64,8,128]{2,1,0:T(8,128)(2,1)} %bitcast.181), calls=%async_computation.1 | async-start | bytes 262144 | tf_op jit(solution)/shard_map/all_to_all | solution.py:167
  26.3 14.2 %copy-start.21 = (f32[1,128]{1,0:T(1,128)}, f32[1,128]{1,0:T(1,128)S(1)}, u32[]{:S(2)}) copy-start(f32[1,128]{1,0:T(1,128)S(1)} %convert_multiply_fusion) | copy-start | bytes 1540
  30.3 30.3 %copy-start.16 = (f32[128,64]{0,1:T(8,128)}, f32[128,64]{0,1:T(8,128)S(1)}, u32[]{:S(2)}) copy-start(f32[128,64]{0,1:T(8,128)S(1)} %get-tuple-element.66) | copy-start | bytes 98308
  40.5 44.8 %copy-start.12 = (bf16[64,8,128]{2,1,0:T(8,128)(2,1)}, bf16[64,8,128]{2,1,0:T(8,128)(2,1)S(1)}, u32[]{:S(2)}) copy-start(bf16[64,8,128]{2,1,0:T(8,128)(2,1)S(1)} %all-to-all-done.1) | copy-start | bytes 393220
  40.5 20.1 %all-to-all-start.5 = ((bf16[64,8,128]{2,1,0:T(8,128)(2,1)}), bf16[64,8,128]{2,1,0:T(8,128)(2,1)S(1)}, u32[]{:S(2)}, u32[]{:S(2)}) async-start(bf16[64,8,128]{2,1,0:T(8,128)(2,1)} %bitcast.182), calls=%async_computation.5 | async-start | bytes 262144 | tf_op jit(solution)/shard_map/all_to_all | solution.py:139
  60.6 19.7 %all-to-all-start.2 = ((bf16[64,8,128]{2,1,0:T(8,128)(2,1)}), bf16[64,8,128]{2,1,0:T(8,128)(2,1)S(1)}, u32[]{:S(2)}, u32[]{:S(2)}) async-start(bf16[64,8,128]{2,1,0:T(8,128)(2,1)} %bitcast.183), calls=%async_computation.2 | async-start | bytes 262144 | tf_op jit(solution)/shard_map/all_to_all | solution.py:166
  65.5 41.4 %copy-start.4 = (f32[128,128]{0,1:T(8,128)}, f32[128,128]{0,1:T(8,128)S(1)}, u32[]{:S(2)}) copy-start(f32[128,128]{0,1:T(8,128)S(1)} %copy.95) | copy-start | bytes 196612
  65.6 41.3 %copy-start.7 = (f32[128,128]{0,1:T(8,128)}, f32[128,128]{0,1:T(8,128)S(1)}, u32[]{:S(2)}) copy-start(f32[128,128]{0,1:T(8,128)S(1)} %copy.96) | copy-start | bytes 196612
  80.3 20.5 %all-to-all-start = ((bf16[64,16,128]{2,1,0:T(8,128)(2,1)}), bf16[64,16,128]{2,1,0:T(8,128)(2,1)S(1)}, u32[]{:S(2)}, u32[]{:S(2)}) async-start(bf16[64,16,128]{2,1,0:T(8,128)(2,1)} %bitcast.4), calls=%async_computation | async-start | bytes 524288 | tf_op jit(solution)/shard_map/all_to_all | solution.py:150
  100.8 20.3 %all-to-all-start.3 = ((bf16[64,8,128]{2,1,0:T(8,128)(2,1)}), bf16[64,8,128]{2,1,0:T(8,128)(2,1)}, u32[]{:S(2)}, u32[]{:S(2)}) async-start(bf16[64,8,128]{2,1,0:T(8,128)(2,1)} %bitcast.21), calls=%async_computation.3 | async-start | bytes 262144 | tf_op jit(solution)/shard_map/all_to_all | solution.py:140
  124.1 2.9 copy-start.6
  130.1 27.3 %copy-start.11 = (bf16[8,64,128]{2,1,0:T(8,128)(2,1)S(1)}, bf16[8,64,128]{2,1,0:T(8,128)(2,1)}, u32[]{:S(2)}) copy-start(bf16[8,64,128]{2,1,0:T(8,128)(2,1)} %get-tuple-element.68) | copy-start | bytes 393220
  131.4 20.6 %all-to-all-start.7 = ((bf16[8,64,128]{2,0,1:T(8,128)(2,1)}), bf16[8,64,128]{2,0,1:T(8,128)(2,1)S(1)}, u32[]{:S(2)}, u32[]{:S(2)}) async-start(bf16[8,64,128]{2,0,1:T(8,128)(2,1)} %copy.126), calls=%async_computation.7 | async-start | bytes 262144 | tf_op jit(solution)/shard_map/all_to_all | solution.py:171
  152.1 19.7 %all-to-all-start.4 = ((bf16[8,64,128]{2,0,1:T(8,128)(2,1)}), bf16[8,64,128]{2,0,1:T(8,128)(2,1)S(1)}, u32[]{:S(2)}, u32[]{:S(2)}) async-start(bf16[8,64,128]{2,0,1:T(8,128)(2,1)} %copy.115), calls=%async_computation.4 | async-start | bytes 262144 | tf_op jit(solution)/shard_map/all_to_all | solution.py:190
  158.8 53.0 %copy-start.17 = (f32[128,64]{0,1:T(8,128)S(1)}, f32[128,64]{0,1:T(8,128)}, u32[]{:S(2)}) copy-start(f32[128,64]{0,1:T(8,128)} %copy-done.16) | copy-start | bytes 98308
  171.7 19.7 %all-to-all-start.6 = ((bf16[8,64,128]{2,0,1:T(8,128)(2,1)}), bf16[8,64,128]{2,0,1:T(8,128)(2,1)S(1)}, u32[]{:S(2)}, u32[]{:S(2)}) async-start(bf16[8,64,128]{2,0,1:T(8,128)(2,1)} %copy.121), calls=%async_computation.6 | async-start | bytes 262144 | tf_op jit(solution)/shard_map/all_to_all | solution.py:191
  176.8 36.1 %copy-start.19 = (f32[128,64]{0,1:T(8,128)S(1)}, f32[128,64]{0,1:T(8,128)}, u32[]{:S(2)}) copy-start(f32[128,64]{0,1:T(8,128)} %get-tuple-element.67) | copy-start | bytes 98308
  177.3 36.1 %copy-start.18 = (f32[64,64]{1,0:T(8,128)S(1)}, f32[64,64]{1,0:T(8,128)}, u32[]{:S(2)}) copy-start(f32[64,64]{1,0:T(8,128)} %param.16) | copy-start | bytes 49156
  177.3 36.1 %copy-start.20 = (f32[128,64]{0,1:T(8,128)S(1)}, f32[128,64]{0,1:T(8,128)}, u32[]{:S(2)}) copy-start(f32[128,64]{0,1:T(8,128)} %get-tuple-element.65) | copy-start | bytes 98308
  177.3 36.4 %copy-start.22 = (f32[1,128]{1,0:T(1,128)S(1)}, f32[1,128]{1,0:T(1,128)}, u32[]{:S(2)}) copy-start(f32[1,128]{1,0:T(1,128)} %copy-done.21) | copy-start | bytes 1540
  177.3 36.6 %copy-start.15 = (f32[128,64]{0,1:T(8,128)S(1)}, f32[128,64]{0,1:T(8,128)}, u32[]{:S(2)}) copy-start(f32[128,64]{0,1:T(8,128)} %copy-done.14) | copy-start | bytes 98308
  191.4 20.4 %all-to-all-start.8 = ((bf16[16,64,128]{2,0,1:T(8,128)(2,1)}), bf16[16,64,128]{2,0,1:T(8,128)(2,1)S(1)}, u32[]{:S(2)}, u32[]{:S(2)}) async-start(bf16[16,64,128]{2,0,1:T(8,128)(2,1)} %copy.135), calls=%async_computation.8 | async-start | bytes 524288 | tf_op jit(solution)/shard_map/all_to_all | solution.py:195
  196.0 452.6 %reduce-scatter.2.cloned.1.call-start = ((), (), s32[]{:S(2)}) async-start(), calls=%async_computation.10 | async-start | bytes 532480 | tf_op jit(solution)/shard_map/reduce_scatter | solution.py:198
  (9 other events, 12.3 us)
Sparse Core Ops, SparseCore 0:
  213.1 435.4 reduce-scatter.1
where the time goes:
time: 658 us; the launch traced here: 657 us
  blocking collectives  429 us (65%)
  waiting for transfers between devices  122 us (19%)
  starting transfers between devices  57.7 us (9%)
  matrix products  18.1 us (3%)
  between operations  14.6 us (2%)
  local copies, waits for them, and re-layouts  8.39 us (1%)
  other arithmetic  7.39 us (1%)
    psum x1, blocking collectives, on_device(): lax.psum((partials[0], partials[1], partials[2], partials[3]), 'seq')  429 us
    all_to_all x1, starting transfers between devices, on_device(): lax.all_to_all(out_cotangent, 'seq', split_axis=0, concat_axis=1, tiled=T...  18.3 us
    all_to_all x1, waiting for transfers between devices, on_device(): lax.all_to_all(filter_grad_ch.astype(jnp.bfloat16), 'seq', split_axis=1,...  15.7 us
    all_to_all x1, waiting for transfers between devices, on_device(): lax.all_to_all(local_filters, 'seq', split_axis=0, concat_axis=1, tiled=T...  14.5 us
    all_to_all x1, waiting for transfers between devices, on_device(): lax.all_to_all(second_grad_ch, 'seq', split_axis=1, concat_axis=0, tiled=...  14 us
    all_to_all x1, waiting for transfers between devices, on_device(): lax.all_to_all(value_branch, 'seq', split_axis=0, concat_axis=1, tiled=True)  13.6 us
    all_to_all x1, waiting for transfers between devices, on_device(): lax.all_to_all(second_gate, 'seq', split_axis=0, concat_axis=1, tiled=True)  13.5 us
  transfers between devices with their start and end apart: 10, of which 10 were waited for; matrix products, arithmetic and copies ran while one was open for 3% of the time, Pallas kernels for 0%

commit v1 on v0

--- a/solution.py
+++ b/solution.py
@@ -5,6 +5,18 @@
 from jax.sharding import PartitionSpec as P
 
 RADIX = 128
+
+
+def _take_wall(m, at_axis, dim_at):
+    return jnp.concatenate(
+        jax.lax.all_to_all(
+            jnp.stack(jnp.split(m, jax.lax.axis_size("seq"), axis=at_axis)),
+            split_axis=0,
+            axis_name="seq",
+            concat_axis=0,
+        ),
+        axis=dim_at,
+    )
 
 
 def make_tables(freq_rows, radix):
@@ -163,7 +175,7 @@
         spectral_product(spec_two, spec_gated, False, False), tables, freq_rows, RADIX
     )
     second_ch, cot_ch = (
-        lax.all_to_all(second_gate, "seq", split_axis=0, concat_axis=1, tiled=True),
+        _take_wall(second_gate, 0, 1),
         lax.all_to_all(out_cotangent, "seq", split_axis=0, concat_axis=1, tiled=True),
     )
     cot_wide = cot_ch.astype(jnp.float32)

time: 658 us -> 741 us (1.13)
  local copies, waits for them, and re-layouts: 8.39 us -> 88.6 us
  starting transfers between devices: 57.7 us -> 67.8 us
  waiting for transfers between devices: 122 us -> 113 us
    unnamed x49 -> x112, local copies, waits for them, and re-layouts: 3.64 us -> 82.6 us
    all_to_all x1, waiting for transfers between devices: 10.2 us -> 0.01 us  [on_device(): lax.all_to_all(out_cotangent, 'seq', split_axis=0, concat_axis=1, tiled=T...]
    all_to_all x1, starting transfers between devices: 5.05 us -> 15.2 us  [on_device(): lax.all_to_all(value_branch, 'seq', split_axis=0, concat_axis=1, tiled=True)]
  transfers between devices with their start and end apart: 10 -> 10, of which waited for: 10 -> 9; matrix products, arithmetic and copies ran while one was open for 3% -> 14% of each run, Pallas kernels for 0% -> 0%
where the time goes in v1:
time: 741 us; the launch traced here: 738 us
  blocking collectives  429 us (58%)
  waiting for transfers between devices  113 us (15%)
  local copies, waits for them, and re-layouts  88.6 us (12%)
  starting transfers between devices  67.8 us (9%)
  matrix products  18.1 us (2%)
  between operations  14.7 us (2%)
  other arithmetic  7.43 us (1%)
    psum x1, blocking collectives, on_device(): lax.psum((partials[0], partials[1], partials[2], partials[3]), 'seq')  429 us
    unnamed x112, local copies, waits for them, and re-layouts  82.6 us
    all_to_all x1, starting transfers between devices, on_device(): lax.all_to_all(out_cotangent, 'seq', split_axis=0, concat_axis=1, tiled=T...  18.3 us
    all_to_all x1, waiting for transfers between devices, on_device(): lax.all_to_all(filter_grad_ch.astype(jnp.bfloat16), 'seq', split_axis=1,...  15.7 us
    all_to_all x1, starting transfers between devices, on_device(): lax.all_to_all(value_branch, 'seq', split_axis=0, concat_axis=1, tiled=True)  15.2 us
  transfers between devices with their start and end apart: 10, of which 9 were waited for; matrix products, arithmetic and copies ran while one was open for 14% of the time, Pallas kernels for 0%

profile of v1, /device:TPU:64, one launch (start us, length us, event | category | flops | bytes accessed | tf_op | source)
XLA Modules:
  0.0 738.4 jit_solution(5329434529734873287)
XLA Ops:
  7.2 18.3 %all-to-all-start.1 = ((bf16[64,8,128]{2,1,0:T(8,128)(2,1)}), bf16[64,8,128]{2,1,0:T(8,128)(2,1)S(1)}, u32[]{:S(2)}, u32[]{:S(2)}) async-start(bf16[64,8,128]{2,1,0:T(8,128)(2,1)} %bitcast.308), calls=%async_computation.1 | async-start | bytes 262144 | tf_op jit(solution)/shard_map/all_to_all | solution.py:179
  107.0 1.6 fusion.148
  109.0 1.6 fusion.149
  110.6 15.2 %all-to-all-start.5 = ((bf16[64,8,128]{2,1,0:T(8,128)(2,1)}), bf16[64,8,128]{2,1,0:T(8,128)(2,1)S(1)}, u32[]{:S(2)}, u32[]{:S(2)}) async-start(bf16[64,8,128]{2,1,0:T(8,128)(2,1)} %bitcast.309), calls=%async_computation.5 | async-start | bytes 262144 | tf_op jit(solution)/shard_map/all_to_all | solution.py:151
  127.3 13.6 %all-to-all-done.5 = bf16[64,8,128]{2,1,0:T(8,128)(2,1)S(1)} async-done(((bf16[64,8,128]{2,1,0:T(8,128)(2,1)}), bf16[64,8,128]{2,1,0:T(8,128)(2,1)S(1)}, u32[]{:S(2)}, u32[]{:S(2)}) %all-to-all-start.5) | async-done | bytes 131104 | tf_op jit(solution)/shard_map/all_to_all | solution.py:151
  140.9 4.6 all-to-all-start.2
  147.1 13.5 %all-to-all-done.2 = bf16[64,8,128]{2,1,0:T(8,128)(2,1)S(1)} async-done(((bf16[64,8,128]{2,1,0:T(8,128)(2,1)}), bf16[64,8,128]{2,1,0:T(8,128)(2,1)S(1)}, u32[]{:S(2)}, u32[]{:S(2)}) %all-to-all-start.2) | async-done | bytes 131104 | tf_op jit(solution)/shard_map/all_to_all | solution.py:12
  160.6 4.6 all-to-all-start
  166.6 14.5 %all-to-all-done = bf16[64,16,128]{2,1,0:T(8,128)(2,1)S(1)} async-done(((bf16[64,16,128]{2,1,0:T(8,128)(2,1)}), bf16[64,16,128]{2,1,0:T(8,128)(2,1)S(1)}, u32[]{:S(2)}, u32[]{:S(2)}) %all-to-all-start) | async-done | bytes 262176 | tf_op jit(solution)/shard_map/all_to_all | solution.py:162
  181.1 5.6 all-to-all-start.3
  190.7 1.3 fusion.17
  192.0 9.4 %all-to-all-done.3 = bf16[64,8,128]{2,1,0:T(8,128)(2,1)} async-done(((bf16[64,8,128]{2,1,0:T(8,128)(2,1)}), bf16[64,8,128]{2,1,0:T(8,128)(2,1)}, u32[]{:S(2)}, u32[]{:S(2)}) %all-to-all-start.3) | async-done | bytes 131104 | tf_op jit(solution)/shard_map/all_to_all | solution.py:152
  201.4 1.4 convolution_bitcast_fusion.1
  205.9 1.3 convolution_bitcast_fusion.3
  211.7 5.6 all-to-all-start.7
  218.4 14.0 %all-to-all-done.7 = bf16[8,64,128]{2,0,1:T(8,128)(2,1)S(1)} async-done(((bf16[8,64,128]{2,0,1:T(8,128)(2,1)}), bf16[8,64,128]{2,0,1:T(8,128)(2,1)S(1)}, u32[]{:S(2)}, u32[]{:S(2)}) %all-to-all-start.7) | async-done | bytes 131104 | tf_op jit(solution)/shard_map/all_to_all | solution.py:183
  232.3 4.6 all-to-all-start.4
  239.1 12.9 %all-to-all-done.4 = bf16[8,64,128]{2,0,1:T(8,128)(2,1)S(1)} async-done(((bf16[8,64,128]{2,0,1:T(8,128)(2,1)}), bf16[8,64,128]{2,0,1:T(8,128)(2,1)S(1)}, u32[]{:S(2)}, u32[]{:S(2)}) %all-to-all-start.4) | async-done | bytes 131104 | tf_op jit(solution)/shard_map/all_to_all | solution.py:202
  252.0 4.6 all-to-all-start.6
  258.7 13.0 %all-to-all-done.6 = bf16[8,64,128]{2,0,1:T(8,128)(2,1)S(1)} async-done(((bf16[8,64,128]{2,0,1:T(8,128)(2,1)}), bf16[8,64,128]{2,0,1:T(8,128)(2,1)S(1)}, u32[]{:S(2)}, u32[]{:S(2)}) %all-to-all-start.6) | async-done | bytes 131104 | tf_op jit(solution)/shard_map/all_to_all | solution.py:203
  271.6 4.6 all-to-all-start.8
  276.3 15.7 %all-to-all-done.8 = bf16[16,64,128]{2,0,1:T(8,128)(2,1)S(1)} async-done(((bf16[16,64,128]{2,0,1:T(8,128)(2,1)}), bf16[16,64,128]{2,0,1:T(8,128)(2,1)S(1)}, u32[]{:S(2)}, u32[]{:S(2)}) %all-to-all-start.8) | async-done | bytes 262176 | tf_op jit(solution)/shard_map/all_to_all | solution.py:207
  294.4 429.2 %all-reduce = (f32[64,33]{0,1:T(8,128)}, f32[64]{0:T(128)}, f32[64,64]{1,0:T(8,128)}, f32[64]{0:T(128)}) all-reduce(f32[64,33]{0,1:T(8,128)S(1)} %fusion.109, f32[64]{0:T(128)S(1)} %get-tuple-element.70, f32[64,64]{1,0:T(8,128)S(1)} %fusion.152, f32[64]{0:T(128)S(1)} %get-tuple-element.72), channel_id=1, replica_groups=mesh['dp'=8,'seq'=64] {'seq'}, use_global_device_ids=true, to_apply=%region_0.1 | all-reduce | flops 6336 | bytes 50688 | tf_op jit(solution)/shard_map/psum | solution.py:215
  723.6 6.0 reduce-scatter.2.cloned.1.call-done
  (175 shorter events, 106.9 us)
Async XLA Ops:
  7.2 119.5 %copy-start = (f32[1024,64]{0,1:T(8,128)S(1)}, f32[1024,64]{0,1:T(8,128)}, u32[]{:S(2)}) copy-start(f32[1024,64]{0,1:T(8,128)} %param.18) | copy-start | bytes 786436
  7.2 103.4 %all-to-all-start.1 = ((bf16[64,8,128]{2,1,0:T(8,128)(2,1)}), bf16[64,8,128]{2,1,0:T(8,128)(2,1)S(1)}, u32[]{:S(2)}, u32[]{:S(2)}) async-start(bf16[64,8,128]{2,1,0:T(8,128)(2,1)} %bitcast.308), calls=%async_computation.1 | async-start | bytes 262144 | tf_op jit(solution)/shard_map/all_to_all | solution.py:179
  26.3 82.7 %copy-start.21 = (f32[1,128]{1,0:T(1,128)}, f32[1,128]{1,0:T(1,128)S(1)}, u32[]{:S(2)}) copy-start(f32[1,128]{1,0:T(1,128)S(1)} %convert_multiply_fusion) | copy-start | bytes 1540
  108.7 51.9 %copy-start.14 = (f32[128,64]{0,1:T(8,128)}, f32[128,64]{0,1:T(8,128)S(1)}, u32[]{:S(2)}) copy-start(f32[128,64]{0,1:T(8,128)S(1)} %get-tuple-element.64) | copy-start | bytes 98308
  110.6 50.0 %copy-start.16 = (f32[128,64]{0,1:T(8,128)}, f32[128,64]{0,1:T(8,128)S(1)}, u32[]{:S(2)}) copy-start(f32[128,64]{0,1:T(8,128)S(1)} %get-tuple-element.66) | copy-start | bytes 98308
  110.6 55.0 %copy-start.12 = (bf16[64,8,128]{2,1,0:T(8,128)(2,1)}, bf16[64,8,128]{2,1,0:T(8,128)(2,1)S(1)}, u32[]{:S(2)}) copy-start(bf16[64,8,128]{2,1,0:T(8,128)(2,1)S(1)} %all-to-all-done.1) | copy-start | bytes 393220
  110.6 30.3 %all-to-all-start.5 = ((bf16[64,8,128]{2,1,0:T(8,128)(2,1)}), bf16[64,8,128]{2,1,0:T(8,128)(2,1)S(1)}, u32[]{:S(2)}, u32[]{:S(2)}) async-start(bf16[64,8,128]{2,1,0:T(8,128)(2,1)} %bitcast.309), calls=%async_computation.5 | async-start | bytes 262144 | tf_op jit(solution)/shard_map/all_to_all | solution.py:151
  140.9 19.7 %all-to-all-start.2 = ((bf16[64,8,128]{2,1,0:T(8,128)(2,1)}), bf16[64,8,128]{2,1,0:T(8,128)(2,1)S(1)}, u32[]{:S(2)}, u32[]{:S(2)}) async-start(bf16[64,8,128]{2,1,0:T(8,128)(2,1)} %constant_dynamic-update-slice_fusion), calls=%async_computation.2 | async-start | bytes 262144 | tf_op jit(solution)/shard_map/all_to_all | solution.py:12
  145.8 41.4 %copy-start.4 = (f32[128,128]{0,1:T(8,128)}, f32[128,128]{0,1:T(8,128)S(1)}, u32[]{:S(2)}) copy-start(f32[128,128]{0,1:T(8,128)S(1)} %copy.158) | copy-start | bytes 196612
  145.9 41.3 %copy-start.7 = (f32[128,128]{0,1:T(8,128)}, f32[128,128]{0,1:T(8,128)S(1)}, u32[]{:S(2)}) copy-start(f32[128,128]{0,1:T(8,128)S(1)} %copy.159) | copy-start | bytes 196612
  160.6 20.5 %all-to-all-start = ((bf16[64,16,128]{2,1,0:T(8,128)(2,1)}), bf16[64,16,128]{2,1,0:T(8,128)(2,1)S(1)}, u32[]{:S(2)}, u32[]{:S(2)}) async-start(bf16[64,16,128]{2,1,0:T(8,128)(2,1)} %bitcast.4), calls=%async_computation | async-start | bytes 524288 | tf_op jit(solution)/shard_map/all_to_all | solution.py:162
  181.1 20.3 %all-to-all-start.3 = ((bf16[64,8,128]{2,1,0:T(8,128)(2,1)}), bf16[64,8,128]{2,1,0:T(8,128)(2,1)}, u32[]{:S(2)}, u32[]{:S(2)}) async-start(bf16[64,8,128]{2,1,0:T(8,128)(2,1)} %bitcast.84), calls=%async_computation.3 | async-start | bytes 262144 | tf_op jit(solution)/shard_map/all_to_all | solution.py:152
  210.5 27.3 %copy-start.11 = (bf16[8,64,128]{2,1,0:T(8,128)(2,1)S(1)}, bf16[8,64,128]{2,1,0:T(8,128)(2,1)}, u32[]{:S(2)}) copy-start(bf16[8,64,128]{2,1,0:T(8,128)(2,1)} %get-tuple-element.68) | copy-start | bytes 393220
  211.7 20.6 %all-to-all-start.7 = ((bf16[8,64,128]{2,0,1:T(8,128)(2,1)}), bf16[8,64,128]{2,0,1:T(8,128)(2,1)S(1)}, u32[]{:S(2)}, u32[]{:S(2)}) async-start(bf16[8,64,128]{2,0,1:T(8,128)(2,1)} %copy.189), calls=%async_computation.7 | async-start | bytes 262144 | tf_op jit(solution)/shard_map/all_to_all | solution.py:183
  232.3 19.6 %all-to-all-start.4 = ((bf16[8,64,128]{2,0,1:T(8,128)(2,1)}), bf16[8,64,128]{2,0,1:T(8,128)(2,1)S(1)}, u32[]{:S(2)}, u32[]{:S(2)}) async-start(bf16[8,64,128]{2,0,1:T(8,128)(2,1)} %copy.178), calls=%async_computation.4 | async-start | bytes 262144 | tf_op jit(solution)/shard_map/all_to_all | solution.py:202
  239.0 53.0 %copy-start.17 = (f32[128,64]{0,1:T(8,128)S(1)}, f32[128,64]{0,1:T(8,128)}, u32[]{:S(2)}) copy-start(f32[128,64]{0,1:T(8,128)} %copy-done.16) | copy-start | bytes 98308
  252.0 19.6 %all-to-all-start.6 = ((bf16[8,64,128]{2,0,1:T(8,128)(2,1)}), bf16[8,64,128]{2,0,1:T(8,128)(2,1)S(1)}, u32[]{:S(2)}, u32[]{:S(2)}) async-start(bf16[8,64,128]{2,0,1:T(8,128)(2,1)} %copy.184), calls=%async_computation.6 | async-start | bytes 262144 | tf_op jit(solution)/shard_map/all_to_all | solution.py:203
  257.1 36.1 %copy-start.19 = (f32[128,64]{0,1:T(8,128)S(1)}, f32[128,64]{0,1:T(8,128)}, u32[]{:S(2)}) copy-start(f32[128,64]{0,1:T(8,128)} %get-tuple-element.67) | copy-start | bytes 98308
  257.6 36.1 %copy-start.18 = (f32[64,64]{1,0:T(8,128)S(1)}, f32[64,64]{1,0:T(8,128)}, u32[]{:S(2)}) copy-start(f32[64,64]{1,0:T(8,128)} %param.16) | copy-start | bytes 49156
  257.6 36.1 %copy-start.20 = (f32[128,64]{0,1:T(8,128)S(1)}, f32[128,64]{0,1:T(8,128)}, u32[]{:S(2)}) copy-start(f32[128,64]{0,1:T(8,128)} %get-tuple-element.65) | copy-start | bytes 98308
  257.6 36.4 %copy-start.22 = (f32[1,128]{1,0:T(1,128)S(1)}, f32[1,128]{1,0:T(1,128)}, u32[]{:S(2)}) copy-start(f32[1,128]{1,0:T(1,128)} %copy-done.21) | copy-start | bytes 1540
  257.6 36.6 %copy-start.15 = (f32[128,64]{0,1:T(8,128)S(1)}, f32[128,64]{0,1:T(8,128)}, u32[]{:S(2)}) copy-start(f32[128,64]{0,1:T(8,128)} %copy-done.14) | copy-start | bytes 98308
  271.6 20.4 %all-to-all-start.8 = ((bf16[16,64,128]{2,0,1:T(8,128)(2,1)}), bf16[16,64,128]{2,0,1:T(8,128)(2,1)S(1)}, u32[]{:S(2)}, u32[]{:S(2)}) async-start(bf16[16,64,128]{2,0,1:T(8,128)(2,1)} %copy.198), calls=%async_computation.8 | async-start | bytes 524288 | tf_op jit(solution)/shard_map/all_to_all | solution.py:207
  276.2 453.3 %reduce-scatter.2.cloned.1.call-start = ((), (), s32[]{:S(2)}) async-start(), calls=%async_computation.10 | async-start | bytes 532480 | tf_op jit(solution)/shard_map/reduce_scatter | solution.py:210
  (9 other events, 14.6 us)
Sparse Core Ops, SparseCore 0:
  293.3 436.2 reduce-scatter.1
